TPU v7x, 512 devices: a whole 4x8x8 slice. The times are simulated.
512 devices in a mesh: inst: 64 (over z_hi, x, y), tp: 8 (over z_lo, core).
Axes of the slice: x: 4, y: 8, z: 8 (z_hi: 2, z_lo: 4; z = z_hi * 4 + z_lo), core: 2. Of those that a mesh axis runs over, the one named last changes fastest.
Arguments:
- step_queries: bfloat16 [4, 512, 8192], P(None, 'inst', 'tp'), may hold values from -11 to 11
- step_keyvals: bfloat16 [4, 512, 8, 256], P(None, 'inst', 'tp'), may hold values from -9.5 to 9.5
- cache_pages: bfloat16 [8192, 16, 8, 256], P('inst', None, 'tp'), may hold values from -9.5 to 9.5
- block_table: int32 [512, 16], P('inst'), may hold values from 0 to 127, as said below
- context_len: int32 [512], replicated, may hold values from 1 to 256, as said below
- partner: int32 [64], replicated, may hold values from 0 to 63, as said below
- moved_slot: int32 [64], replicated, may hold values from 0 to 7
- prompt_queries: bfloat16 [32768, 8192], P(('inst', 'tp')), may hold values from -11 to 11
- prompt_keyvals: bfloat16 [32768, 8, 256], P(('inst', 'tp')), may hold values from -9.5 to 9.5
- prompt_target: int32 [32768, 1], replicated, may hold values from 0 to 63; in each aligned block of 64 rows (0 to 63, 64 to 127, ...) at most 2 rows name the same one
Outputs:
- decode_output: bfloat16 [4, 512, 8192], P(None, 'inst', 'tp')
- prefill_output: bfloat16 [65536, 8192], P('inst', 'tp')
Inputs may be any that keep to these rules, and one draw needn't show every extreme that they name: partner[partner[i]] = i, and i and partner[i] differ in exactly one bit. `block_table`: the 8 rows of one instance together name each of its 128 pages once. `context_len`: some request holds exactly 256 tokens. `prompt_target`: among the 64 rows of one device no instance is named more than 2 times.
All inputs are finite; a program needn't handle non-finite values.
Results may differ from a plain program's by a relative error of at most 0.0049.
Values may be sent and summed in bfloat16 or wider, within the bound.
No kernel may reach another device: no remote copies, remote signals or barrier semaphores. Data moves between devices by JAX's collectives and lax.ppermute only.
A program may use at most 64 MiB of HBM per device.

v0:
```python
import jax
import jax.numpy as jnp
from jax import lax
from jax.sharding import PartitionSpec as P


def swapped(array, axis, bit):
    return lax.ppermute(array, axis, [(i, i ^ 1 << bit) for i in range(lax.axis_size(axis))])


def masked_weights(scores, mask):
    shifted = jnp.where(mask, scores, jnp.float32(-1e30))
    top = jnp.max(shifted, axis=-1, keepdims=True)
    expo = jnp.where(mask, jnp.exp(shifted - top), jnp.float32(0.0))
    total = jnp.sum(expo, axis=-1, keepdims=True)
    total = jnp.where(total > 0, total, jnp.float32(1.0))
    return expo / total


def decode_block(queries, context, lengths, fresh):
    steps, count, width = queries.shape
    kv_heads = context.shape[2]
    head_dim = context.shape[3] // 2
    group = width // (kv_heads * head_dim)
    span = context.shape[1]
    scale = head_dim ** (-0.5)
    query = queries.reshape(steps, count, kv_heads, group, head_dim)
    past = (
        jnp.einsum(
            "trkgd,rckd->trkgc", query, context[..., :head_dim], preferred_element_type=jnp.float32
        )
        * scale
    )
    newer = (
        jnp.einsum(
            "trkgd,urkd->trkgu", query, fresh[..., :head_dim], preferred_element_type=jnp.float32
        )
        * scale
    )
    past_mask = (jnp.arange(span, dtype=jnp.int32)[None, :] < lengths[:, None])[
        None, :, None, None, :
    ]
    step_ids = jnp.arange(steps, dtype=jnp.int32)
    new_mask = (step_ids[None, :] <= step_ids[:, None])[:, None, None, None, :]
    mask = jnp.concatenate(
        [jnp.broadcast_to(past_mask, past.shape), jnp.broadcast_to(new_mask, newer.shape)], axis=-1
    )
    weights = masked_weights(jnp.concatenate([past, newer], axis=-1), mask).astype(jnp.bfloat16)
    out = jnp.einsum(
        "trkgc,rckd->trkgd",
        weights[..., :span],
        context[..., head_dim:],
        preferred_element_type=jnp.float32,
    )
    out = out + jnp.einsum(
        "trkgu,urkd->trkgd",
        weights[..., span:],
        fresh[..., head_dim:],
        preferred_element_type=jnp.float32,
    )
    return out.reshape(steps, count, width).astype(jnp.bfloat16)


def prefill_block(queries, keyvals, valid):
    slots, width = queries.shape
    kv_heads = keyvals.shape[1]
    head_dim = keyvals.shape[2] // 2
    group = width // (kv_heads * head_dim)
    scale = head_dim ** (-0.5)
    query = queries.reshape(slots, kv_heads, group, head_dim)
    block = 512
    pieces = []
    for start in range(0, slots, block):
        finish = start + block
        scores = (
            jnp.einsum(
                "qkgd,ckd->kgqc",
                query[start:finish],
                keyvals[:finish, :, :head_dim],
                preferred_element_type=jnp.float32,
            )
            * scale
        )
        query_pos = jnp.arange(start, finish, dtype=jnp.int32)
        key_pos = jnp.arange(finish, dtype=jnp.int32)
        mask = (valid[None, :finish] & (key_pos[None, :] <= query_pos[:, None]))[None, None]
        weights = masked_weights(scores, jnp.broadcast_to(mask, scores.shape)).astype(jnp.bfloat16)
        out = jnp.einsum(
            "kgqc,ckd->qkgd",
            weights,
            keyvals[:finish, :, head_dim:],
            preferred_element_type=jnp.float32,
        )
        out = jnp.where(valid[start:finish, None, None, None], out, jnp.float32(0.0))
        pieces.append(out.reshape(block, width).astype(jnp.bfloat16))
    return jnp.concatenate(pieces, axis=0)


def local(
    step_queries,
    step_keyvals,
    cache_pages,
    block_table,
    context_len,
    partner,
    moved_slot,
    prompt_queries,
    prompt_keyvals,
    prompt_target,
):
    inst_count = lax.axis_size("inst")
    tp_count = lax.axis_size("tp")
    me_inst = lax.axis_index("inst")
    me_tp = lax.axis_index("tp")
    requests = block_table.shape[0]
    kv_heads = step_keyvals.shape[2]
    head_dim = step_keyvals.shape[3] // 2
    rows_dev = prompt_queries.shape[0]
    capacity = max(2, 2 * rows_dev // inst_count)
    devices = inst_count * tp_count
    targets = prompt_target[:, 0].reshape(devices, rows_dev)
    mine = lax.dynamic_index_in_dim(targets, me_inst * tp_count + me_tp, 0, keepdims=False)
    onehot = (mine[:, None] == jnp.arange(inst_count, dtype=jnp.int32)[None, :]).astype(jnp.int32)
    rank = jnp.sum((jnp.cumsum(onehot, axis=0) - onehot) * onehot, axis=1)
    place = mine * capacity + rank
    dispatch = (
        jnp.arange(inst_count * capacity, dtype=jnp.int32)[:, None] == place[None, :]
    ).astype(jnp.bfloat16)
    send_queries = (
        jnp.dot(dispatch, prompt_queries, preferred_element_type=jnp.float32)
        .astype(jnp.bfloat16)
        .reshape(inst_count, capacity, -1)
    )
    flat_keyvals = prompt_keyvals.reshape(rows_dev, -1)
    send_keyvals = (
        jnp.dot(dispatch, flat_keyvals, preferred_element_type=jnp.float32)
        .astype(jnp.bfloat16)
        .reshape(inst_count, capacity, -1)
    )
    recv_queries, recv_keyvals = (
        lax.all_to_all(
            lax.all_to_all(send_queries, "inst", split_axis=0, concat_axis=0, tiled=True),
            "tp",
            split_axis=2,
            concat_axis=1,
            tiled=True,
        ),
        lax.all_to_all(
            lax.all_to_all(send_keyvals, "inst", split_axis=0, concat_axis=0, tiled=True),
            "tp",
            split_axis=2,
            concat_axis=1,
            tiled=True,
        ),
    )
    gathered = cache_pages[block_table]
    context = gathered.reshape(requests, -1, kv_heads, 2 * head_dim)
    lengths = lax.dynamic_slice_in_dim(context_len, me_inst * requests, requests)
    my_slot = moved_slot[me_inst]
    other = partner[me_inst]
    other_len = context_len[other * requests + moved_slot[other]]
    bit_total = inst_count.bit_length() - 1
    distance = jnp.bitwise_xor(me_inst, other)
    outgoing = lax.dynamic_index_in_dim(context, my_slot, 0, keepdims=False)
    incoming = outgoing
    for bit in range(bit_total):
        arrived = swapped(outgoing, "inst", bit)
        incoming = jnp.where(distance == 1 << bit, arrived, incoming)
    context = lax.dynamic_update_index_in_dim(context, incoming, my_slot, 0)
    lengths = lengths.at[my_slot].set(other_len)
    decode_output = decode_block(step_queries, context, lengths, step_keyvals)
    slots = inst_count * tp_count * capacity
    slot_queries = recv_queries.reshape(slots, -1)
    slot_keyvals = recv_keyvals.reshape(slots, kv_heads, 2 * head_dim)
    counts = jnp.sum((targets == me_inst).astype(jnp.int32), axis=1)
    valid = (jnp.arange(capacity, dtype=jnp.int32)[None, :] < counts[:, None]).reshape(slots)
    prefill_output = prefill_block(slot_queries, slot_keyvals, valid)
    return (decode_output, prefill_output)


def solution(mesh):
    placed = (
        P(None, "inst", "tp"),
        P(None, "inst", "tp", None),
        P("inst", None, "tp", None),
        P("inst", None),
        P(),
        P(),
        P(),
        P(("inst", "tp"), None),
        P(("inst", "tp"), None, None),
        P(),
    )
    return jax.shard_map(
        local,
        mesh=mesh,
        in_specs=placed,
        out_specs=(P(None, "inst", "tp"), P("inst", "tp")),
        check_vma=False,
    )
```

profile of v0, /device:TPU:1, one launch (start us, length us, event | category | flops | bytes accessed | tf_op | source)
XLA Modules:
  0.0 244.2 jit_solution(7322671740194920094)
XLA Ops:
  6.0 20.0 %all-to-all-start = ((bf16[64,2,2048]{2,1,0:T(2,128)(2,1)}), bf16[64,2,2048]{2,1,0:T(2,128)(2,1)}, u32[]{:S(2)}, u32[]{:S(2)}) async-start(bf16[64,2,2048]{2,1,0:T(2,128)(2,1)} %reshape.492), calls=%async_computation | async-start | bytes 1048576 | tf_op jit(solution)/shard_map/all_to_all | solution.py:149
  26.6 2.6 %reshape.496 = bf16[64,2,8192]{2,1,0:T(2,128)(2,1)} reshape(bf16[128,8192]{1,0:T(8,128)(2,1)S(1)} %convolution_convert_fusion) | data formatting | bytes 4194304 | tf_op jit(solution)/shard_map/reshape | solution.py:132
  29.3 17.0 %all-to-all-done = bf16[64,2,2048]{2,1,0:T(2,128)(2,1)} async-done(((bf16[64,2,2048]{2,1,0:T(2,128)(2,1)}), bf16[64,2,2048]{2,1,0:T(2,128)(2,1)}, u32[]{:S(2)}, u32[]{:S(2)}) %all-to-all-start) | async-done | bytes 524320 | tf_op jit(solution)/shard_map/all_to_all | solution.py:149
  46.2 6.5 %all-to-all-start.2 = ((bf16[64,2,8192]{2,1,0:T(2,128)(2,1)}), bf16[64,2,8192]{2,1,0:T(2,128)(2,1)S(1)}, u32[]{:S(2)}, u32[]{:S(2)}) async-start(bf16[64,2,8192]{2,1,0:T(2,128)(2,1)} %reshape.496), calls=%async_computation.2 | async-start | bytes 4194304 | tf_op jit(solution)/shard_map/all_to_all | solution.py:142
  56.8 48.4 %all-to-all-done.2 = bf16[64,2,8192]{2,1,0:T(2,128)(2,1)S(1)} async-done(((bf16[64,2,8192]{2,1,0:T(2,128)(2,1)}), bf16[64,2,8192]{2,1,0:T(2,128)(2,1)S(1)}, u32[]{:S(2)}, u32[]{:S(2)}) %all-to-all-start.2) | async-done | bytes 2097184 | tf_op jit(solution)/shard_map/all_to_all | solution.py:142
  105.3 7.9 %all-to-all-start.1 = ((bf16[8,2,16384]{2,1,0:T(2,128)(2,1)}), bf16[8,2,16384]{2,1,0:T(2,128)(2,1)S(1)}, u32[]{:S(2)}, u32[]{:S(2)}) async-start(bf16[8,2,16384]{2,1,0:T(2,128)(2,1)} %reshape.536), calls=%async_computation.1 | async-start | bytes 1048576 | tf_op jit(solution)/shard_map/all_to_all | solution.py:148
  117.6 7.7 %copy.69 = bf16[64,2,8192]{0,1,2:T(2,128)(2,1)} copy(bf16[64,2,8192]{2,1,0:T(2,128)(2,1)S(1)} %all-to-all-done.2) | data formatting | bytes 4194304 | tf_op jit(solution)/shard_map/all_to_all | solution.py:142
  125.3 7.6 %reshape.534 = bf16[8,2,65536]{2,1,0:T(2,128)(2,1)} reshape(bf16[8192,2,64]{2,1,0:T(2,128)(2,1)} %bitcast.160) | data formatting | bytes 4194304
  132.9 5.1 %all-to-all-start.3 = ((bf16[8,2,65536]{2,1,0:T(2,128)(2,1)}), bf16[8,2,65536]{2,1,0:T(2,128)(2,1)}, u32[]{:S(2)}, u32[]{:S(2)}) async-start(bf16[8,2,65536]{2,1,0:T(2,128)(2,1)} %reshape.534), calls=%async_computation.3 | async-start | bytes 4194304 | tf_op jit(solution)/shard_map/all_to_all | solution.py:141
  140.7 3.7 %collective-permute-start = (bf16[256,1,256]{2,0,1:T(8,128)(2,1)S(1)}, bf16[256,1,256]{2,0,1:T(8,128)(2,1)S(1)}, u32[]{:S(2)}, u32[]{:S(2)}) collective-permute-start(bf16[256,1,256]{2,0,1:T(8,128)(2,1)S(1)} %dynamic-slice_bitcast_fusion), channel_id=1, source_target_pairs={{0,256},{8,264},{16,272},{24,280},{32,288},{40,296},{48,304},{56,3... | collective-permute-start | bytes 393224 | tf_op jit(solution)/shard_map/ppermute | solution.py:8
  144.4 3.3 %collective-permute-start.1 = (bf16[256,1,256]{2,0,1:T(8,128)(2,1)S(1)}, bf16[256,1,256]{2,0,1:T(8,128)(2,1)S(1)}, u32[]{:S(2)}, u32[]{:S(2)}) collective-permute-start(bf16[256,1,256]{2,0,1:T(8,128)(2,1)S(1)} %dynamic-slice_bitcast_fusion), channel_id=1, source_target_pairs={{0,128},{8,136},{16,144},{24,152},{32,160},{40,168},{48,176},{56,1... | collective-permute-start | bytes 393224 | tf_op jit(solution)/shard_map/ppermute | solution.py:8
  149.7 3.7 %collective-permute-start.3 = (bf16[256,1,256]{2,0,1:T(8,128)(2,1)S(1)}, bf16[256,1,256]{2,0,1:T(8,128)(2,1)S(1)}, u32[]{:S(2)}, u32[]{:S(2)}) collective-permute-start(bf16[256,1,256]{2,0,1:T(8,128)(2,1)S(1)} %dynamic-slice_bitcast_fusion), channel_id=1, source_target_pairs={{0,32},{8,40},{16,48},{24,56},{32,0},{40,8},{48,16},{56,24},{64,96... | collective-permute-start | bytes 393224 | tf_op jit(solution)/shard_map/ppermute | solution.py:8
  153.3 4.0 %collective-permute-start.4 = (bf16[256,1,256]{2,0,1:T(8,128)(2,1)S(1)}, bf16[256,1,256]{2,0,1:T(8,128)(2,1)}, u32[]{:S(2)}, u32[]{:S(2)}) collective-permute-start(bf16[256,1,256]{2,0,1:T(8,128)(2,1)S(1)} %dynamic-slice_bitcast_fusion), channel_id=1, source_target_pairs={{0,16},{8,24},{16,0},{24,8},{32,48},{40,56},{48,32},{56,40},{64,80... | collective-permute-start | bytes 393224 | tf_op jit(solution)/shard_map/ppermute | solution.py:8
  160.2 20.3 %collective-permute-done = bf16[256,1,256]{2,0,1:T(8,128)(2,1)S(1)} collective-permute-done((bf16[256,1,256]{2,0,1:T(8,128)(2,1)S(1)}, bf16[256,1,256]{2,0,1:T(8,128)(2,1)S(1)}, u32[]{:S(2)}, u32[]{:S(2)}) %collective-permute-start) | collective-permute-done | bytes 131104 | tf_op jit(solution)/shard_map/ppermute | solution.py:8
  180.5 3.6 %collective-permute-start.5 = (bf16[256,1,256]{2,0,1:T(8,128)(2,1)S(1)}, bf16[256,1,256]{2,0,1:T(8,128)(2,1)S(1)}, u32[]{:S(2)}, u32[]{:S(2)}) collective-permute-start(bf16[256,1,256]{2,0,1:T(8,128)(2,1)S(1)} %dynamic-slice_bitcast_fusion), channel_id=1, source_target_pairs={{0,8},{8,0},{16,24},{24,16},{32,40},{40,32},{48,56},{56,48},{64,72... | collective-permute-start | bytes 393224 | tf_op jit(solution)/shard_map/ppermute | solution.py:8
  189.6 3.0 %reshape.537 = bf16[2048,2,64]{2,1,0:T(2,128)(2,1)S(1)} reshape(bf16[8,2,16384]{2,1,0:T(2,128)(2,1)} %copy-done.2) | data formatting | bytes 1048576
  193.6 7.4 %reshape.535 = bf16[8192,2,64]{2,1,0:T(2,128)(2,1)} reshape(bf16[8,2,65536]{2,1,0:T(2,128)(2,1)} %all-to-all-done.3) | data formatting | bytes 4194304
  201.0 11.1 %copy.70 = bf16[64,2,8,1024]{3,1,2,0:T(2,128)(2,1)} copy(bf16[64,2,8,1024]{0,1,3,2:T(2,128)(2,1)} %bitcast.161) | data formatting | bytes 4194304 | tf_op jit(solution)/shard_map/all_to_all | solution.py:141
  212.1 4.0 %fusion.40 = (bf16[32,8,2,1024]{3,2,1,0:T(2,128)(2,1)S(1)}, bf16[32,8,2,1024]{3,2,1,0:T(2,128)(2,1)}) fusion(bf16[64,8,2,1024]{3,2,1,0:T(2,128)(2,1)} %bitcast.162), kind=kLoop, calls=%fused_computation.86 | loop fusion | bytes 4194304 | tf_op jit(solution)/shard_map/slice | solution.py:78
  220.5 2.9 %fusion.10 = bf16[1,128,8,512]{3,1,2,0:T(8,128)(2,1)S(1)} fusion(f32[8,512]{1,0:T(8,128)S(1)} %compare_select_fusion.1, f32[8,512]{1,0:T(8,128)S(1)} %get-tuple-element.32, f32[512,512,8]{1,0,2:T(8,128)S(1)} %get-tuple-element.33, pred[512,512]{0,1:T(8,128)(4,1)S(1)} %fusion.24, pred[512]{0:T(512)(128)(4,1)S(1)} %copy-done.7, ...), kind=kOutput, calls=%fused_computation.22 | convolution fusion | flops 550502400 | bytes 9863680 | tf_op jit(solution)/shard_map/kgqc,ckd->qkgd/dot_general | solution.py:88
  225.7 3.0 %fusion = (f32[8,512]{1,0:T(8,128)S(1)}, f32[1024,512,8]{1,0,2:T(8,128)S(1)}) fusion(pred[512,1024]{0,1:T(8,128)(4,1)S(1)} %fusion.11, bf16[512,8,128]{2,1,0:T(8,128)(2,1)S(1)} %reshape.501, bf16[1024,1,256]{2,0,1:T(8,128)(2,1)S(1)} %reshape.493), kind=kOutput, calls=%fused_computation.4 | convolution fusion | flops 1086320640 | bytes 18628608 | tf_op jit(solution)/shard_map/qkgd,ckd->kgqc/dot_general | solution.py:76
  228.7 4.2 %fusion.1 = f32[8,512]{1,0:T(8,128)S(1)} fusion(f32[1024,512,8]{1,0,2:T(8,128)S(1)} %get-tuple-element.31, f32[8,512]{1,0:T(8,128)S(1)} %get-tuple-element.30, pred[512,1024]{0,1:T(8,128)(4,1)S(1)} %fusion.11), kind=kLoop, calls=%fused_computation.5 | loop fusion | flops 20967424 | bytes 17334272 | tf_op jit(solution)/shard_map/reduce_sum | solution.py:15
  233.0 6.3 %fusion.9 = bf16[1,128,8,512]{3,1,2,0:T(8,128)(2,1)} fusion(f32[8,512]{1,0:T(8,128)S(1)} %compare_select_fusion, f32[8,512]{1,0:T(8,128)S(1)} %get-tuple-element.30, f32[1024,512,8]{1,0,2:T(8,128)S(1)} %get-tuple-element.31, pred[512,1024]{0,1:T(8,128)(4,1)S(1)} %fusion.11, pred[512]{0:T(512)(128)(4,1)S(1)} %broadcast_in_dim.121, ...), kind=kOutput, calls=%fused_computation.20 | convolution fusion | flops 1099956224 | bytes 18645504 | tf_op jit(solution)/shard_map/kgqc,ckd->qkgd/dot_general | solution.py:88
  241.5 2.7 %pad_maximum_fusion = bf16[1024,1024]{1,0:T(8,128)(2,1)} fusion(bf16[512,1024]{1,0:T(8,128)(2,1)} %copy.78, bf16[512,1024]{1,0:T(8,128)(2,1)S(1)} %copy.77), kind=kLoop, calls=%fused_computation.18 | loop fusion | flops 4194304 | bytes 4194304 | tf_op jit(solution)/shard_map/concatenate | solution.py:96
  (88 shorter events, 31.3 us)
Async XLA Ops:
  0.6 25.3 %copy-start = (bf16[64,8192]{1,0:T(8,128)(2,1)S(1)}, bf16[64,8192]{1,0:T(8,128)(2,1)}, u32[]{:S(2)}) copy-start(bf16[64,8192]{1,0:T(8,128)(2,1)} %param.19) | copy-start | bytes 3145732
  6.0 107.2 %copy-start.10 = (s32[64]{0:T(128)S(1)}, s32[64]{0:T(128)}, u32[]{:S(2)}) copy-start(s32[64]{0:T(128)} %param.17) | copy-start | bytes 772
  6.0 109.7 %copy-start.8 = (s32[64]{0:T(128)S(1)}, s32[64]{0:T(128)}, u32[]{:S(2)}) copy-start(s32[64]{0:T(128)} %param.18) | copy-start | bytes 772
  6.0 40.3 %all-to-all-start = ((bf16[64,2,2048]{2,1,0:T(2,128)(2,1)}), bf16[64,2,2048]{2,1,0:T(2,128)(2,1)}, u32[]{:S(2)}, u32[]{:S(2)}) async-start(bf16[64,2,2048]{2,1,0:T(2,128)(2,1)} %reshape.492), calls=%async_computation | async-start | bytes 1048576 | tf_op jit(solution)/shard_map/all_to_all | solution.py:149
  46.2 59.0 %all-to-all-start.2 = ((bf16[64,2,8192]{2,1,0:T(2,128)(2,1)}), bf16[64,2,8192]{2,1,0:T(2,128)(2,1)S(1)}, u32[]{:S(2)}, u32[]{:S(2)}) async-start(bf16[64,2,8192]{2,1,0:T(2,128)(2,1)} %reshape.496), calls=%async_computation.2 | async-start | bytes 4194304 | tf_op jit(solution)/shard_map/all_to_all | solution.py:142
  105.3 27.7 %all-to-all-start.1 = ((bf16[8,2,16384]{2,1,0:T(2,128)(2,1)}), bf16[8,2,16384]{2,1,0:T(2,128)(2,1)S(1)}, u32[]{:S(2)}, u32[]{:S(2)}) async-start(bf16[8,2,16384]{2,1,0:T(2,128)(2,1)} %reshape.536), calls=%async_computation.1 | async-start | bytes 1048576 | tf_op jit(solution)/shard_map/all_to_all | solution.py:148
  117.6 20.4 %copy-start.5 = (s32[8,16]{1,0:T(8,128)S(1)}, s32[8,16]{1,0:T(8,128)}, u32[]{:S(2)}) copy-start(s32[8,16]{1,0:T(8,128)} %param.15) | copy-start | bytes 1540
  117.6 42.0 %copy-start.4 = (bf16[4,8,1,256]{3,1,2,0:T(8,128)(2,1)S(1)}, bf16[4,8,1,256]{3,1,2,0:T(8,128)(2,1)}, u32[]{:S(2)}) copy-start(bf16[4,8,1,256]{3,1,2,0:T(8,128)(2,1)} %param.13) | copy-start | bytes 49156
  125.3 34.0 %copy-start.9 = (s32[512]{0:T(512)S(1)}, s32[512]{0:T(512)}, u32[]{:S(2)}) copy-start(s32[512]{0:T(512)} %param.16) | copy-start | bytes 6148
  125.3 59.6 %copy-start.3 = (bf16[4,8,1024]{2,1,0:T(8,128)(2,1)S(1)}, bf16[4,8,1024]{2,1,0:T(8,128)(2,1)}, u32[]{:S(2)}) copy-start(bf16[4,8,1024]{2,1,0:T(8,128)(2,1)} %param.12) | copy-start | bytes 196612
  132.9 54.5 %copy-start.2 = (bf16[8,2,16384]{2,1,0:T(2,128)(2,1)}, bf16[8,2,16384]{2,1,0:T(2,128)(2,1)S(1)}, u32[]{:S(2)}) copy-start(bf16[8,2,16384]{2,1,0:T(2,128)(2,1)S(1)} %all-to-all-done.1) | copy-start | bytes 1572868
  132.9 60.6 %all-to-all-start.3 = ((bf16[8,2,65536]{2,1,0:T(2,128)(2,1)}), bf16[8,2,65536]{2,1,0:T(2,128)(2,1)}, u32[]{:S(2)}, u32[]{:S(2)}) async-start(bf16[8,2,65536]{2,1,0:T(2,128)(2,1)} %reshape.534), calls=%async_computation.3 | async-start | bytes 4194304 | tf_op jit(solution)/shard_map/all_to_all | solution.py:141
  140.7 39.8 %collective-permute-start = (bf16[256,1,256]{2,0,1:T(8,128)(2,1)S(1)}, bf16[256,1,256]{2,0,1:T(8,128)(2,1)S(1)}, u32[]{:S(2)}, u32[]{:S(2)}) collective-permute-start(bf16[256,1,256]{2,0,1:T(8,128)(2,1)S(1)} %dynamic-slice_bitcast_fusion), channel_id=1, source_target_pairs={{0,256},{8,264},{16,272},{24,280},{32,288},{40,296},{48,304},{56,3... | collective-permute-start | bytes 393224 | tf_op jit(solution)/shard_map/ppermute | solution.py:8
  144.4 40.7 %collective-permute-start.1 = (bf16[256,1,256]{2,0,1:T(8,128)(2,1)S(1)}, bf16[256,1,256]{2,0,1:T(8,128)(2,1)S(1)}, u32[]{:S(2)}, u32[]{:S(2)}) collective-permute-start(bf16[256,1,256]{2,0,1:T(8,128)(2,1)S(1)} %dynamic-slice_bitcast_fusion), channel_id=1, source_target_pairs={{0,128},{8,136},{16,144},{24,152},{32,160},{40,168},{48,176},{56,1... | collective-permute-start | bytes 393224 | tf_op jit(solution)/shard_map/ppermute | solution.py:8
  147.7 37.3 %collective-permute-start.2 = (bf16[256,1,256]{2,0,1:T(8,128)(2,1)S(1)}, bf16[256,1,256]{2,0,1:T(8,128)(2,1)S(1)}, u32[]{:S(2)}, u32[]{:S(2)}) collective-permute-start(bf16[256,1,256]{2,0,1:T(8,128)(2,1)S(1)} %dynamic-slice_bitcast_fusion), channel_id=1, source_target_pairs={{0,64},{8,72},{16,80},{24,88},{32,96},{40,104},{48,112},{56,120},{... | collective-permute-start | bytes 393224 | tf_op jit(solution)/shard_map/ppermute | solution.py:8
  149.7 35.4 %collective-permute-start.3 = (bf16[256,1,256]{2,0,1:T(8,128)(2,1)S(1)}, bf16[256,1,256]{2,0,1:T(8,128)(2,1)S(1)}, u32[]{:S(2)}, u32[]{:S(2)}) collective-permute-start(bf16[256,1,256]{2,0,1:T(8,128)(2,1)S(1)} %dynamic-slice_bitcast_fusion), channel_id=1, source_target_pairs={{0,32},{8,40},{16,48},{24,56},{32,0},{40,8},{48,16},{56,24},{64,96... | collective-permute-start | bytes 393224 | tf_op jit(solution)/shard_map/ppermute | solution.py:8
  153.3 31.8 %collective-permute-start.4 = (bf16[256,1,256]{2,0,1:T(8,128)(2,1)S(1)}, bf16[256,1,256]{2,0,1:T(8,128)(2,1)}, u32[]{:S(2)}, u32[]{:S(2)}) collective-permute-start(bf16[256,1,256]{2,0,1:T(8,128)(2,1)S(1)} %dynamic-slice_bitcast_fusion), channel_id=1, source_target_pairs={{0,16},{8,24},{16,0},{24,8},{32,48},{40,56},{48,32},{56,40},{64,80... | collective-permute-start | bytes 393224 | tf_op jit(solution)/shard_map/ppermute | solution.py:8
  159.3 25.6 %copy-start.6 = (pred[512]{0:T(512)(128)(4,1)}, pred[512]{0:T(512)(128)(4,1)S(1)}, u32[]{:S(2)}) copy-start(pred[512]{0:T(512)(128)(4,1)S(1)} %broadcast_in_dim.114) | copy-start | bytes 1540
  180.5 7.0 %collective-permute-start.5 = (bf16[256,1,256]{2,0,1:T(8,128)(2,1)S(1)}, bf16[256,1,256]{2,0,1:T(8,128)(2,1)S(1)}, u32[]{:S(2)}, u32[]{:S(2)}) collective-permute-start(bf16[256,1,256]{2,0,1:T(8,128)(2,1)S(1)} %dynamic-slice_bitcast_fusion), channel_id=1, source_target_pairs={{0,8},{8,0},{16,24},{24,16},{32,40},{40,32},{48,56},{56,48},{64,72... | collective-permute-start | bytes 393224 | tf_op jit(solution)/shard_map/ppermute | solution.py:8
  216.8 3.7 %copy-start.7 = (pred[512]{0:T(512)(128)(4,1)S(1)}, pred[512]{0:T(512)(128)(4,1)}, u32[]{:S(2)}) copy-start(pred[512]{0:T(512)(128)(4,1)} %copy-done.6) | copy-start | bytes 1540
  233.0 11.2 %copy-start.1 = (bf16[64,8192]{1,0:T(8,128)(2,1)S(1)}, bf16[64,8192]{1,0:T(8,128)(2,1)}, u32[]{:S(2)}) copy-start(bf16[64,8192]{1,0:T(8,128)(2,1)} %param.19) | copy-start | bytes 3145732
where the time goes:
time: 246 us; the launch traced here: 244 us
  waiting for transfers between devices  88 us (36%)
  local copies, waits for them, and re-layouts  61.1 us (25%)
  starting transfers between devices  59.7 us (24%)
  matrix products  15.5 us (6%)
  other arithmetic  13 us (5%)
  between operations  6.95 us (3%)
    all_to_all x1, waiting for transfers between devices, local(): lax.all_to_all(send_queries, 'inst', split_axis=0, concat_axis=0, tiled=T...  48.4 us
    ppermute x6, waiting for transfers between devices, swapped(): lax.ppermute(array, axis, [(i, i ^ 1 << bit) for i in range(lax.axis_size...  22.6 us
    unnamed x29, local copies, waits for them, and re-layouts  21.7 us
    ppermute x6, starting transfers between devices, swapped(): lax.ppermute(array, axis, [(i, i ^ 1 << bit) for i in range(lax.axis_size...  20.2 us
    all_to_all x1, starting transfers between devices, local(): lax.all_to_all(send_keyvals, 'inst', split_axis=0, concat_axis=0, tiled=T...  20 us
    all_to_all x1, waiting for transfers between devices, local(): lax.all_to_all(send_keyvals, 'inst', split_axis=0, concat_axis=0, tiled=T...  17 us
    all_to_all x1, local copies, waits for them, and re-layouts, local(): lax.all_to_all(lax.all_to_all(send_queries, 'inst', split_axis=0, concat_...  11.1 us
    dot_general x2, matrix products, prefill_block(): jnp.einsum('kgqc,ckd->qkgd', weights, keyvals[:finish, :, head_dim:], pre...  9.18 us
  transfers between devices with their start and end apart: 10, of which 4 were waited for; matrix products, arithmetic and copies ran while one was open for 14% of the time, Pallas kernels for 0%

commit v1 on v0

--- a/solution.py
+++ b/solution.py
@@ -2,6 +2,13 @@
 import jax.numpy as jnp
 from jax import lax
 from jax.sharding import PartitionSpec as P
+
+
+def trade_parts(x, axis, split, join):
+    count = lax.axis_size(axis)
+    tiles = jnp.stack(jnp.split(x, count, axis=split), axis=0)
+    tiles = lax.all_to_all(tiles, axis, split_axis=0, concat_axis=0)
+    return jnp.concatenate(tiles, axis=join)
 
 
 def swapped(array, axis, bit):
@@ -138,12 +145,11 @@
         .reshape(inst_count, capacity, -1)
     )
     recv_queries, recv_keyvals = (
-        lax.all_to_all(
+        trade_parts(
             lax.all_to_all(send_queries, "inst", split_axis=0, concat_axis=0, tiled=True),
             "tp",
-            split_axis=2,
-            concat_axis=1,
-            tiled=True,
+            2,
+            1,
         ),
         lax.all_to_all(
             lax.all_to_all(send_keyvals, "inst", split_axis=0, concat_axis=0, tiled=True),

time: 246 us -> 230 us (0.935)
  local copies, waits for them, and re-layouts: 61.1 us -> 45.6 us
    all_to_all x2 -> x0, local copies, waits for them, and re-layouts: 18.8 us -> none  [the longest x1 11.1 us: local(): lax.all_to_all(lax.all_to_all(send_queries, 'inst', split_axis=0, concat_...]
    all_to_all x1, waiting for transfers between devices: 48.4 us -> 40.6 us  [local(): lax.all_to_all(send_queries, 'inst', split_axis=0, concat_axis=0, tiled=T...]
    all_to_all x1, waiting for transfers between devices: 0.01 us -> 7.21 us  [local(): lax.all_to_all(lax.all_to_all(send_keyvals, 'inst', split_axis=0, concat_...]
    unnamed x29 -> x32, local copies, waits for them, and re-layouts: 21.7 us -> 15.5 us
    slice x1 -> x3, local copies, waits for them, and re-layouts: 4.03 us -> 7.71 us  [prefill_block(): query[start:finish]]
  transfers between devices with their start and end apart: 10 -> 10, of which waited for: 4 -> 5; matrix products, arithmetic and copies ran while one was open for 14% -> 14% of each run, Pallas kernels for 0% -> 0%
where the time goes in v1:
time: 230 us; the launch traced here: 229 us
  waiting for transfers between devices  86.8 us (38%)
  starting transfers between devices  59.7 us (26%)
  local copies, waits for them, and re-layouts  45.6 us (20%)
  matrix products  16.3 us (7%)
  other arithmetic  13.7 us (6%)
  between operations  6.89 us (3%)
    all_to_all x1, waiting for transfers between devices, local(): lax.all_to_all(send_queries, 'inst', split_axis=0, concat_axis=0, tiled=T...  40.6 us
    ppermute x6, waiting for transfers between devices, swapped(): lax.ppermute(array, axis, [(i, i ^ 1 << bit) for i in range(lax.axis_size...  22.1 us
    ppermute x6, starting transfers between devices, swapped(): lax.ppermute(array, axis, [(i, i ^ 1 << bit) for i in range(lax.axis_size...  20.2 us
    all_to_all x1, starting transfers between devices, local(): lax.all_to_all(send_keyvals, 'inst', split_axis=0, concat_axis=0, tiled=T...  19.8 us
    all_to_all x1, waiting for transfers between devices, local(): lax.all_to_all(send_keyvals, 'inst', split_axis=0, concat_axis=0, tiled=T...  16.9 us
    unnamed x32, local copies, waits for them, and re-layouts  15.5 us
    dot_general x2, matrix products, prefill_block(): jnp.einsum('kgqc,ckd->qkgd', weights, keyvals[:finish, :, head_dim:], pre...  10 us
    all_to_all x1, starting transfers between devices, local(): lax.all_to_all(lax.all_to_all(send_keyvals, 'inst', split_axis=0, concat_...  8.19 us
  transfers between devices with their start and end apart: 10, of which 5 were waited for; matrix products, arithmetic and copies ran while one was open for 14% of the time, Pallas kernels for 0%

profile of v1, /device:TPU:1, one launch (start us, length us, event | category | flops | bytes accessed | tf_op | source)
XLA Modules:
  0.0 229.0 jit_solution(15939527978129002294)
XLA Ops:
  6.0 19.8 %all-to-all-start = ((bf16[64,2,2048]{2,1,0:T(2,128)(2,1)}), bf16[64,2,2048]{2,1,0:T(2,128)(2,1)}, u32[]{:S(2)}, u32[]{:S(2)}) async-start(bf16[64,2,2048]{2,1,0:T(2,128)(2,1)} %reshape.494), calls=%async_computation | async-start | bytes 1048576 | tf_op jit(solution)/shard_map/all_to_all | solution.py:155
  26.5 2.6 %reshape.498 = bf16[64,2,8192]{2,1,0:T(2,128)(2,1)} reshape(bf16[128,8192]{1,0:T(8,128)(2,1)S(1)} %convolution_convert_fusion) | data formatting | bytes 4194304 | tf_op jit(solution)/shard_map/reshape | solution.py:139
  29.1 16.9 %all-to-all-done = bf16[64,2,2048]{2,1,0:T(2,128)(2,1)} async-done(((bf16[64,2,2048]{2,1,0:T(2,128)(2,1)}), bf16[64,2,2048]{2,1,0:T(2,128)(2,1)}, u32[]{:S(2)}, u32[]{:S(2)}) %all-to-all-start) | async-done | bytes 524320 | tf_op jit(solution)/shard_map/all_to_all | solution.py:155
  46.1 6.4 %all-to-all-start.2 = ((bf16[64,2,8192]{2,1,0:T(2,128)(2,1)}), bf16[64,2,8192]{2,1,0:T(2,128)(2,1)S(1)}, u32[]{:S(2)}, u32[]{:S(2)}) async-start(bf16[64,2,8192]{2,1,0:T(2,128)(2,1)} %reshape.498), calls=%async_computation.2 | async-start | bytes 4194304 | tf_op jit(solution)/shard_map/all_to_all | solution.py:149
  56.9 3.7 %copy.74 = bf16[64,2,2048]{0,1,2:T(2,128)(2,1)} copy(bf16[64,2,2048]{2,1,0:T(2,128)(2,1)} %all-to-all-done) | data formatting | bytes 1048576 | tf_op jit(solution)/shard_map/all_to_all | solution.py:155
  60.7 3.8 %reshape.537 = bf16[8,2,16384]{2,1,0:T(2,128)(2,1)} reshape(bf16[2048,2,64]{2,1,0:T(2,128)(2,1)} %bitcast.189) | data formatting | bytes 1048576
  64.5 40.6 %all-to-all-done.2 = bf16[64,2,8192]{2,1,0:T(2,128)(2,1)S(1)} async-done(((bf16[64,2,8192]{2,1,0:T(2,128)(2,1)}), bf16[64,2,8192]{2,1,0:T(2,128)(2,1)S(1)}, u32[]{:S(2)}, u32[]{:S(2)}) %all-to-all-start.2) | async-done | bytes 2097184 | tf_op jit(solution)/shard_map/all_to_all | solution.py:149
  105.1 8.2 %all-to-all-start.1 = ((bf16[8,2,16384]{2,1,0:T(2,128)(2,1)}), bf16[8,2,16384]{2,1,0:T(2,128)(2,1)}, u32[]{:S(2)}, u32[]{:S(2)}) async-start(bf16[8,2,16384]{2,1,0:T(2,128)(2,1)} %reshape.537), calls=%async_computation.1 | async-start | bytes 1048576 | tf_op jit(solution)/shard_map/all_to_all | solution.py:154
  120.7 7.2 %all-to-all-done.1 = bf16[8,2,16384]{2,1,0:T(2,128)(2,1)} async-done(((bf16[8,2,16384]{2,1,0:T(2,128)(2,1)}), bf16[8,2,16384]{2,1,0:T(2,128)(2,1)}, u32[]{:S(2)}, u32[]{:S(2)}) %all-to-all-start.1) | async-done | bytes 524320 | tf_op jit(solution)/shard_map/all_to_all | solution.py:154
  127.9 5.1 %all-to-all-start.3 = ((bf16[8,64,2,1024]{3,2,1,0:T(2,128)(2,1)}), bf16[8,64,2,1024]{3,2,1,0:T(2,128)(2,1)}, u32[]{:S(2)}, u32[]{:S(2)}) async-start(bf16[8,64,2,1024]{3,2,1,0:T(2,128)(2,1)} %fusion.25), calls=%async_computation.3 | async-start | bytes 4194304 | tf_op jit(solution)/shard_map/all_to_all | solution.py:10
  135.6 3.3 %collective-permute-start = (bf16[256,1,256]{2,0,1:T(8,128)(2,1)S(1)}, bf16[256,1,256]{2,0,1:T(8,128)(2,1)S(1)}, u32[]{:S(2)}, u32[]{:S(2)}) collective-permute-start(bf16[256,1,256]{2,0,1:T(8,128)(2,1)S(1)} %dynamic-slice_bitcast_fusion), channel_id=1, source_target_pairs={{0,256},{8,264},{16,272},{24,280},{32,288},{40,296},{48,304},{56,3... | collective-permute-start | bytes 393224 | tf_op jit(solution)/shard_map/ppermute | solution.py:15
  138.9 3.3 %collective-permute-start.1 = (bf16[256,1,256]{2,0,1:T(8,128)(2,1)S(1)}, bf16[256,1,256]{2,0,1:T(8,128)(2,1)}, u32[]{:S(2)}, u32[]{:S(2)}) collective-permute-start(bf16[256,1,256]{2,0,1:T(8,128)(2,1)S(1)} %dynamic-slice_bitcast_fusion), channel_id=1, source_target_pairs={{0,128},{8,136},{16,144},{24,152},{32,160},{40,168},{48,176},{56,1... | collective-permute-start | bytes 393224 | tf_op jit(solution)/shard_map/ppermute | solution.py:15
  144.2 4.3 %collective-permute-start.3 = (bf16[256,1,256]{2,0,1:T(8,128)(2,1)S(1)}, bf16[256,1,256]{2,0,1:T(8,128)(2,1)}, u32[]{:S(2)}, u32[]{:S(2)}) collective-permute-start(bf16[256,1,256]{2,0,1:T(8,128)(2,1)S(1)} %dynamic-slice_bitcast_fusion), channel_id=1, source_target_pairs={{0,32},{8,40},{16,48},{24,56},{32,0},{40,8},{48,16},{56,24},{64,96... | collective-permute-start | bytes 393224 | tf_op jit(solution)/shard_map/ppermute | solution.py:15
  148.5 3.6 %collective-permute-start.4 = (bf16[256,1,256]{2,0,1:T(8,128)(2,1)S(1)}, bf16[256,1,256]{2,0,1:T(8,128)(2,1)}, u32[]{:S(2)}, u32[]{:S(2)}) collective-permute-start(bf16[256,1,256]{2,0,1:T(8,128)(2,1)S(1)} %dynamic-slice_bitcast_fusion), channel_id=1, source_target_pairs={{0,16},{8,24},{16,0},{24,8},{32,48},{40,56},{48,32},{56,40},{64,80... | collective-permute-start | bytes 393224 | tf_op jit(solution)/shard_map/ppermute | solution.py:15
  154.9 20.1 %collective-permute-done = bf16[256,1,256]{2,0,1:T(8,128)(2,1)S(1)} collective-permute-done((bf16[256,1,256]{2,0,1:T(8,128)(2,1)S(1)}, bf16[256,1,256]{2,0,1:T(8,128)(2,1)S(1)}, u32[]{:S(2)}, u32[]{:S(2)}) %collective-permute-start) | collective-permute-done | bytes 131104 | tf_op jit(solution)/shard_map/ppermute | solution.py:15
  175.0 3.8 %collective-permute-start.5 = (bf16[256,1,256]{2,0,1:T(8,128)(2,1)S(1)}, bf16[256,1,256]{2,0,1:T(8,128)(2,1)S(1)}, u32[]{:S(2)}, u32[]{:S(2)}) collective-permute-start(bf16[256,1,256]{2,0,1:T(8,128)(2,1)S(1)} %dynamic-slice_bitcast_fusion), channel_id=1, source_target_pairs={{0,8},{8,0},{16,24},{24,16},{32,40},{40,32},{48,56},{56,48},{64,72... | collective-permute-start | bytes 393224 | tf_op jit(solution)/shard_map/ppermute | solution.py:15
  184.8 3.0 %reshape.538 = bf16[2048,2,64]{2,1,0:T(2,128)(2,1)S(1)} reshape(bf16[8,2,16384]{2,1,0:T(2,128)(2,1)} %all-to-all-done.1) | data formatting | bytes 1048576
  189.6 3.5 %fusion.48 = (bf16[32,8,2,1024]{3,2,0,1:T(2,128)(2,1)S(1)}, bf16[32,8,2,1024]{3,2,0,1:T(2,128)(2,1)}) fusion(bf16[64,8,2,1024]{3,2,0,1:T(2,128)(2,1)} %bitcast.47), kind=kLoop, calls=%fused_computation.102 | loop fusion | bytes 4194304 | tf_op jit(solution)/shard_map/slice | solution.py:85
  200.6 3.7 %fusion.10 = bf16[1,128,8,512]{3,1,2,0:T(8,128)(2,1)} fusion(f32[8,512]{1,0:T(8,128)S(1)} %compare_select_fusion.1, f32[8,512]{1,0:T(8,128)S(1)} %get-tuple-element.32, f32[512,512,8]{1,0,2:T(8,128)S(1)} %get-tuple-element.33, pred[512,512]{0,1:T(8,128)(4,1)S(1)} %fusion.24, pred[512]{0:T(512)(128)(4,1)S(1)} %broadcast_in_dim.114, ...), kind=kOutput, calls=%fused_computation.22 | convolution fusion | flops 550502400 | bytes 9863680 | tf_op jit(solution)/shard_map/kgqc,ckd->qkgd/dot_general | solution.py:95
  210.7 3.0 %fusion = (f32[8,512]{1,0:T(8,128)S(1)}, f32[1024,512,8]{1,0,2:T(8,128)S(1)}) fusion(pred[512,1024]{0,1:T(8,128)(4,1)S(1)} %fusion.11, bf16[512,8,128]{2,1,0:T(8,128)(2,1)S(1)} %reshape.504, bf16[1024,1,256]{2,0,1:T(8,128)(2,1)S(1)} %copy-done.3), kind=kOutput, calls=%fused_computation.4 | convolution fusion | flops 1086320640 | bytes 18628608 | tf_op jit(solution)/shard_map/qkgd,ckd->kgqc/dot_general | solution.py:83
  213.7 4.0 %fusion.1 = f32[8,512]{1,0:T(8,128)S(1)} fusion(f32[1024,512,8]{1,0,2:T(8,128)S(1)} %get-tuple-element.31, f32[8,512]{1,0:T(8,128)S(1)} %get-tuple-element.30, pred[512,1024]{0,1:T(8,128)(4,1)S(1)} %fusion.11), kind=kLoop, calls=%fused_computation.5 | loop fusion | flops 20967424 | bytes 17334272 | tf_op jit(solution)/shard_map/reduce_sum | solution.py:22
  217.7 6.3 %fusion.9 = bf16[1,128,8,512]{3,1,2,0:T(8,128)(2,1)} fusion(f32[8,512]{1,0:T(8,128)S(1)} %compare_select_fusion, f32[8,512]{1,0:T(8,128)S(1)} %get-tuple-element.30, f32[1024,512,8]{1,0,2:T(8,128)S(1)} %get-tuple-element.31, pred[512,1024]{0,1:T(8,128)(4,1)S(1)} %fusion.11, pred[512]{0:T(512)(128)(4,1)S(1)} %broadcast_in_dim.121, ...), kind=kOutput, calls=%fused_computation.20 | convolution fusion | flops 1099956224 | bytes 18645504 | tf_op jit(solution)/shard_map/kgqc,ckd->qkgd/dot_general | solution.py:95
  224.0 2.3 copy.85
  226.3 2.7 %pad_maximum_fusion = bf16[1024,1024]{1,0:T(8,128)(2,1)} fusion(bf16[512,1024]{1,0:T(8,128)(2,1)} %copy.85, bf16[512,1024]{1,0:T(8,128)(2,1)S(1)} %copy-done.1), kind=kLoop, calls=%fused_computation.18 | loop fusion | flops 4194304 | bytes 4194304 | tf_op jit(solution)/shard_map/concatenate | solution.py:103
  (92 shorter events, 40.9 us)
Async XLA Ops:
  0.6 25.2 %copy-start = (bf16[64,8192]{1,0:T(8,128)(2,1)S(1)}, bf16[64,8192]{1,0:T(8,128)(2,1)}, u32[]{:S(2)}) copy-start(bf16[64,8192]{1,0:T(8,128)(2,1)} %param.19) | copy-start | bytes 3145732
  6.0 40.1 %all-to-all-start = ((bf16[64,2,2048]{2,1,0:T(2,128)(2,1)}), bf16[64,2,2048]{2,1,0:T(2,128)(2,1)}, u32[]{:S(2)}, u32[]{:S(2)}) async-start(bf16[64,2,2048]{2,1,0:T(2,128)(2,1)} %reshape.494), calls=%async_computation | async-start | bytes 1048576 | tf_op jit(solution)/shard_map/all_to_all | solution.py:155
  26.5 26.0 %copy-start.9 = (s32[64]{0:T(128)S(1)}, s32[64]{0:T(128)}, u32[]{:S(2)}) copy-start(s32[64]{0:T(128)} %param.17) | copy-start | bytes 772
  26.5 28.5 %copy-start.7 = (s32[64]{0:T(128)S(1)}, s32[64]{0:T(128)}, u32[]{:S(2)}) copy-start(s32[64]{0:T(128)} %param.18) | copy-start | bytes 772
  46.1 59.0 %all-to-all-start.2 = ((bf16[64,2,8192]{2,1,0:T(2,128)(2,1)}), bf16[64,2,8192]{2,1,0:T(2,128)(2,1)S(1)}, u32[]{:S(2)}, u32[]{:S(2)}) async-start(bf16[64,2,8192]{2,1,0:T(2,128)(2,1)} %reshape.498), calls=%async_computation.2 | async-start | bytes 4194304 | tf_op jit(solution)/shard_map/all_to_all | solution.py:149
  105.1 22.8 %all-to-all-start.1 = ((bf16[8,2,16384]{2,1,0:T(2,128)(2,1)}), bf16[8,2,16384]{2,1,0:T(2,128)(2,1)}, u32[]{:S(2)}, u32[]{:S(2)}) async-start(bf16[8,2,16384]{2,1,0:T(2,128)(2,1)} %reshape.537), calls=%async_computation.1 | async-start | bytes 1048576 | tf_op jit(solution)/shard_map/all_to_all | solution.py:154
  113.2 19.7 %copy-start.6 = (s32[8,16]{1,0:T(8,128)S(1)}, s32[8,16]{1,0:T(8,128)}, u32[]{:S(2)}) copy-start(s32[8,16]{1,0:T(8,128)} %param.15) | copy-start | bytes 1540
  118.8 35.2 %copy-start.8 = (s32[512]{0:T(512)S(1)}, s32[512]{0:T(512)}, u32[]{:S(2)}) copy-start(s32[512]{0:T(512)} %param.16) | copy-start | bytes 6148
  118.8 35.5 %copy-start.5 = (bf16[4,8,1,256]{3,1,2,0:T(8,128)(2,1)S(1)}, bf16[4,8,1,256]{3,1,2,0:T(8,128)(2,1)}, u32[]{:S(2)}) copy-start(bf16[4,8,1,256]{3,1,2,0:T(8,128)(2,1)} %param.13) | copy-start | bytes 49156
  119.7 59.9 %copy-start.4 = (bf16[4,8,1024]{2,1,0:T(8,128)(2,1)S(1)}, bf16[4,8,1024]{2,1,0:T(8,128)(2,1)}, u32[]{:S(2)}) copy-start(bf16[4,8,1024]{2,1,0:T(8,128)(2,1)} %param.12) | copy-start | bytes 196612
  127.9 61.7 %all-to-all-start.3 = ((bf16[8,64,2,1024]{3,2,1,0:T(2,128)(2,1)}), bf16[8,64,2,1024]{3,2,1,0:T(2,128)(2,1)}, u32[]{:S(2)}, u32[]{:S(2)}) async-start(bf16[8,64,2,1024]{3,2,1,0:T(2,128)(2,1)} %fusion.25), calls=%async_computation.3 | async-start | bytes 4194304 | tf_op jit(solution)/shard_map/all_to_all | solution.py:10
  135.6 39.4 %collective-permute-start = (bf16[256,1,256]{2,0,1:T(8,128)(2,1)S(1)}, bf16[256,1,256]{2,0,1:T(8,128)(2,1)S(1)}, u32[]{:S(2)}, u32[]{:S(2)}) collective-permute-start(bf16[256,1,256]{2,0,1:T(8,128)(2,1)S(1)} %dynamic-slice_bitcast_fusion), channel_id=1, source_target_pairs={{0,256},{8,264},{16,272},{24,280},{32,288},{40,296},{48,304},{56,3... | collective-permute-start | bytes 393224 | tf_op jit(solution)/shard_map/ppermute | solution.py:15
  138.9 40.8 %collective-permute-start.1 = (bf16[256,1,256]{2,0,1:T(8,128)(2,1)S(1)}, bf16[256,1,256]{2,0,1:T(8,128)(2,1)}, u32[]{:S(2)}, u32[]{:S(2)}) collective-permute-start(bf16[256,1,256]{2,0,1:T(8,128)(2,1)S(1)} %dynamic-slice_bitcast_fusion), channel_id=1, source_target_pairs={{0,128},{8,136},{16,144},{24,152},{32,160},{40,168},{48,176},{56,1... | collective-permute-start | bytes 393224 | tf_op jit(solution)/shard_map/ppermute | solution.py:15
  142.2 37.5 %collective-permute-start.2 = (bf16[256,1,256]{2,0,1:T(8,128)(2,1)S(1)}, bf16[256,1,256]{2,0,1:T(8,128)(2,1)}, u32[]{:S(2)}, u32[]{:S(2)}) collective-permute-start(bf16[256,1,256]{2,0,1:T(8,128)(2,1)S(1)} %dynamic-slice_bitcast_fusion), channel_id=1, source_target_pairs={{0,64},{8,72},{16,80},{24,88},{32,96},{40,104},{48,112},{56,120},{... | collective-permute-start | bytes 393224 | tf_op jit(solution)/shard_map/ppermute | solution.py:15
  144.2 35.6 %collective-permute-start.3 = (bf16[256,1,256]{2,0,1:T(8,128)(2,1)S(1)}, bf16[256,1,256]{2,0,1:T(8,128)(2,1)}, u32[]{:S(2)}, u32[]{:S(2)}) collective-permute-start(bf16[256,1,256]{2,0,1:T(8,128)(2,1)S(1)} %dynamic-slice_bitcast_fusion), channel_id=1, source_target_pairs={{0,32},{8,40},{16,48},{24,56},{32,0},{40,8},{48,16},{56,24},{64,96... | collective-permute-start | bytes 393224 | tf_op jit(solution)/shard_map/ppermute | solution.py:15
  148.5 31.3 %collective-permute-start.4 = (bf16[256,1,256]{2,0,1:T(8,128)(2,1)S(1)}, bf16[256,1,256]{2,0,1:T(8,128)(2,1)}, u32[]{:S(2)}, u32[]{:S(2)}) collective-permute-start(bf16[256,1,256]{2,0,1:T(8,128)(2,1)S(1)} %dynamic-slice_bitcast_fusion), channel_id=1, source_target_pairs={{0,16},{8,24},{16,0},{24,8},{32,48},{40,56},{48,32},{56,40},{64,80... | collective-permute-start | bytes 393224 | tf_op jit(solution)/shard_map/ppermute | solution.py:15
  175.0 6.7 %collective-permute-start.5 = (bf16[256,1,256]{2,0,1:T(8,128)(2,1)S(1)}, bf16[256,1,256]{2,0,1:T(8,128)(2,1)S(1)}, u32[]{:S(2)}, u32[]{:S(2)}) collective-permute-start(bf16[256,1,256]{2,0,1:T(8,128)(2,1)S(1)} %dynamic-slice_bitcast_fusion), channel_id=1, source_target_pairs={{0,8},{8,0},{16,24},{24,16},{32,40},{40,32},{48,56},{56,48},{64,72... | collective-permute-start | bytes 393224 | tf_op jit(solution)/shard_map/ppermute | solution.py:15
  189.6 7.4 %copy-start.3 = (bf16[1024,1,256]{2,0,1:T(8,128)(2,1)S(1)}, bf16[1024,1,256]{2,0,1:T(8,128)(2,1)}, u32[]{:S(2)}) copy-start(bf16[1024,1,256]{2,0,1:T(8,128)(2,1)} %reshape.495) | copy-start | bytes 1572868
  200.6 6.0 %copy-start.2 = (bf16[32,8,2,1024]{3,2,0,1:T(2,128)(2,1)S(1)}, bf16[32,8,2,1024]{3,2,0,1:T(2,128)(2,1)}, u32[]{:S(2)}) copy-start(bf16[32,8,2,1024]{3,2,0,1:T(2,128)(2,1)} %get-tuple-element.23) | copy-start | bytes 3145732
  217.7 8.6 %copy-start.1 = (bf16[512,1024]{1,0:T(8,128)(2,1)S(1)}, bf16[512,1024]{1,0:T(8,128)(2,1)}, u32[]{:S(2)}) copy-start(bf16[512,1024]{1,0:T(8,128)(2,1)} %copy.84) | copy-start | bytes 3145732
